TPU v7x, 256 devices: a whole 4x4x8 slice. The times are simulated.
256 devices in a mesh: seq: 32 (over y, z_hi, x), grp: 8 (over z_lo, core).
Axes of the slice: x: 4, y: 4, z: 8 (z_hi: 2, z_lo: 4; z = z_hi * 4 + z_lo), core: 2. Of those that a mesh axis runs over, the one named last changes fastest.
Arguments:
- inputs: bfloat16 [4096, 8192], P('seq', 'grp'), may hold values from -10 to 10
- query_states: bfloat16 [4096, 8192], P('seq', 'grp'), may hold values from -12 to 12
- key_states: bfloat16 [4096, 1024], P('seq', 'grp'), may hold values from -6 to 6
- value_states: bfloat16 [4096, 1024], P('seq', 'grp'), may hold values from -6 to 6
- doc_ids: int32 [4096], replicated, may hold values from 0 to 7, never falling along the last dimension, each value on 1 to 3072 neighbouring positions
- modality: int32 [4096], P('seq'), may hold values from 0 to 1, as said below
- expert_ids: int32 [4096, 4], P('seq'), may hold values from -1 to 31, as said below
- norm_gain: float32 [8192], P('grp'), may hold values from 0.1 to 1.9
- router_w: bfloat16 [8192, 64], P('grp'), may hold values from -0.0625 to 0.0625
- w_in: bfloat16 [2, 32, 8192, 1408], P(None, 'seq', 'grp'), may hold values from -1 to 1
- w_out: bfloat16 [2, 32, 1408, 8192], P(None, 'seq', None, 'grp'), may hold values from -2 to 2
- grad_out: bfloat16 [4096, 8192], P('seq', 'grp'), may hold values from -12 to 12
Outputs:
- layer_out: bfloat16 [4096, 8192], P('seq', 'grp')
- state_grad: bfloat16 [4096, 8192], P('seq', 'grp')
Inputs may be any that keep to these rules, and one draw needn't show every extreme that they name: Modality is constant over aligned runs of 16 tokens; every block of 128 tokens held by one index of seq has a run of each modality. `expert_ids`: -1 marks an empty choice; the other entries of a token are distinct experts of its modality. At most 16 choices of the 128 tokens of one index of seq name one expert of one modality, and in every draw one text expert and one image expert are named by exactly 16 choices of every such block.
All inputs are finite; a program needn't handle non-finite values.
Results may differ from a plain program's by a relative error of at most 0.008.
Values may be sent and summed in bfloat16 or wider, within the bound.
A program may use at most 128 MiB of HBM per device.

v0:
```python
import jax
import jax.numpy as jnp
from jax import lax
from jax.sharding import PartitionSpec as P

D = 8192
HEADS = 64
KV_HEADS = 8
HEAD_DIM = 128
FF = 1408
TOP = 4
CAP = 16
eps_norm = 1e-05
gate_offset = 0.5


def gelu_back(pre_act, grad_in):
    return jax.vjp(lambda inner: jax.nn.gelu(inner, approximate=True), pre_act)[1](grad_in)[0]


def row_total(partial_value):
    return lax.psum(partial_value, "grp")


def dispatch(buffers):
    return lax.all_to_all(buffers, "seq", split_axis=1, concat_axis=1, tiled=True)


def collect(buffers):
    return lax.all_to_all(buffers, "seq", split_axis=1, concat_axis=1, tiled=True)


def hidden_step(partial_value, finish):
    summed = lax.psum(partial_value.astype(jnp.bfloat16), "grp").astype(jnp.float32)
    return finish(summed)


def attend(query_states, key_states, value_states, doc_ids):
    length = query_states.shape[0]
    kv_local = key_states.shape[1] // HEAD_DIM
    group_size = HEADS // KV_HEADS
    query_heads = query_states.reshape(length, kv_local, group_size, HEAD_DIM)
    first_query = lax.axis_index("seq") * length
    query_pos = first_query + jnp.arange(length, dtype=jnp.int32)
    query_doc = lax.dynamic_slice_in_dim(doc_ids, first_query, length)
    score_scale = HEAD_DIM ** (-0.5)
    key_piece = lax.all_gather(key_states, "seq", axis=0, tiled=True)
    value_piece = lax.all_gather(value_states, "seq", axis=0, tiled=True)
    piece_rows = key_piece.shape[0]
    best_score = jnp.full((length, kv_local, group_size), -1e30, jnp.float32)
    key_heads = key_piece.reshape(piece_rows, kv_local, HEAD_DIM)
    value_heads = value_piece.reshape(piece_rows, kv_local, HEAD_DIM).astype(jnp.float32)
    scores = (
        jnp.einsum("qhgd,khd->qhgk", query_heads, key_heads, preferred_element_type=jnp.float32)
        * score_scale
    )
    key_pos = jnp.arange(piece_rows, dtype=jnp.int32)
    allowed = (key_pos[None, :] <= query_pos[:, None]) & (doc_ids[None, :] == query_doc[:, None])
    allowed = allowed[:, None, None, :]
    scores = jnp.where(allowed, scores, -1e30)
    new_best = jnp.maximum(best_score, jnp.max(scores, axis=3))
    weights = jnp.where(allowed, jnp.exp(scores - new_best[..., None]), 0.0)
    totals = jnp.sum(weights, axis=3)
    summed = jnp.einsum("qhgk,khd->qhgd", weights, value_heads, precision=lax.Precision.HIGHEST)
    best_score, totals, summed = (new_best, totals, summed)
    return (
        (summed / totals[..., None])
        .reshape(length, kv_local * group_size * HEAD_DIM)
        .astype(jnp.bfloat16)
    )


def body(
    inputs,
    query_states,
    key_states,
    value_states,
    doc_ids,
    modality,
    expert_ids,
    norm_gain,
    router_w,
    w_in,
    w_out,
    grad_out,
):
    length, width_local = inputs.shape
    experts = lax.axis_size("seq")
    slot_total = 2 * experts * CAP
    attended = attend(query_states, key_states, value_states, doc_ids)
    resid_state = (inputs.astype(jnp.float32) + attended.astype(jnp.float32)).astype(jnp.bfloat16)
    state_wide = resid_state.astype(jnp.float32)
    squares = row_total(jnp.sum(state_wide * state_wide, axis=1))
    inv_rms = lax.rsqrt(squares / D + eps_norm)[:, None]
    scaled = state_wide * norm_gain[None, :]
    normed = (scaled * inv_rms).astype(jnp.bfloat16)
    logits = row_total(jnp.dot(normed, router_w, preferred_element_type=jnp.float32))
    kept_mask = expert_ids >= 0
    kept_wide = kept_mask.astype(jnp.float32)
    column = modality[:, None] * experts + jnp.where(kept_mask, expert_ids, 0)
    one_hot = (
        column[:, :, None] == jnp.arange(2 * experts, dtype=jnp.int32)[None, None, :]
    ) & kept_mask[:, :, None]
    chosen = jnp.sum(jnp.where(one_hot, logits[:, None, :], 0.0), axis=2)
    lifted = jax.nn.sigmoid(chosen)
    denominator = gate_offset + jnp.sum(kept_wide * lifted, axis=1, keepdims=True)
    gates = kept_wide * lifted / denominator
    entries = length * TOP
    flat_hot = one_hot.reshape(entries, 2 * experts).astype(jnp.bfloat16)
    entry_range = jnp.arange(entries, dtype=jnp.int32)
    earlier = (entry_range[:, None] > entry_range[None, :]).astype(jnp.bfloat16)
    before = jnp.dot(earlier, flat_hot, preferred_element_type=jnp.float32)
    slot_rank = jnp.sum(before * flat_hot.astype(jnp.float32), axis=1).astype(jnp.int32)
    slot_index = column.reshape(entries) * CAP + slot_rank
    table = (
        slot_index[:, None] == jnp.arange(slot_total, dtype=jnp.int32)[None, :]
    ) & kept_mask.reshape(entries)[:, None]
    table = table.astype(jnp.bfloat16).reshape(length, TOP, slot_total)
    token_table = jnp.sum(table, axis=1)
    w_in_local = w_in[:, 0]
    w_out_local = w_out[:, 0]
    sent_rows = jnp.einsum("ts,td->sd", token_table, normed, preferred_element_type=jnp.float32)
    sent_rows = sent_rows.astype(jnp.bfloat16).reshape(2, experts, CAP, width_local)
    got_rows = dispatch(sent_rows)
    partial_value = jnp.einsum(
        "ohn,ons->ohs",
        got_rows.reshape(2, experts * CAP, width_local),
        w_in_local,
        preferred_element_type=jnp.float32,
    ).reshape(2, experts, CAP, FF)

    def forward_finish(pre_act):
        return (jax.nn.gelu(pre_act, approximate=True).astype(jnp.bfloat16), pre_act)

    active, saved_pre = hidden_step(partial_value, forward_finish)
    expert_out = jnp.einsum(
        "nuv,nvg->nug",
        active.reshape(2, experts * CAP, FF),
        w_out_local,
        preferred_element_type=jnp.float32,
    ).astype(jnp.bfloat16)
    returned = collect(expert_out.reshape(2, experts, CAP, width_local)).reshape(
        slot_total, width_local
    )
    entry_out = jnp.einsum("tks,sd->tkd", table, returned, preferred_element_type=jnp.float32)
    mixture = jnp.sum(gates[:, :, None] * entry_out, axis=1)
    layer_out = (state_wide + mixture).astype(jnp.bfloat16)
    grad_wide = grad_out.astype(jnp.float32)
    gate_grad = row_total(jnp.sum(grad_wide[:, None, :] * entry_out, axis=2))
    gate_dot = jnp.sum(gates * gate_grad, axis=1, keepdims=True)
    logit_grad = kept_wide * (gate_grad - gate_dot) / denominator * lifted * (1.0 - lifted)
    logit_full = jnp.sum(jnp.where(one_hot, logit_grad[:, :, None], 0.0), axis=1)
    router_grad = jnp.dot(
        logit_full, router_w.astype(jnp.float32).T, precision=lax.Precision.HIGHEST
    )
    slot_gate = jnp.einsum(
        "tks,tk->s", table.astype(jnp.float32), gates, precision=lax.Precision.HIGHEST
    )
    grad_rows = (
        jnp.einsum("ts,td->sd", token_table, grad_out, preferred_element_type=jnp.float32)
        * slot_gate[:, None]
    )
    grad_rows = grad_rows.astype(jnp.bfloat16).reshape(2, experts, CAP, width_local)
    got_grads = dispatch(grad_rows)
    partial_back = jnp.einsum(
        "ukx,utx->ukt",
        got_grads.reshape(2, experts * CAP, width_local),
        w_out_local,
        preferred_element_type=jnp.float32,
    ).reshape(2, experts, CAP, FF)

    def backward_finish(act_grad):
        return (gelu_back(saved_pre, act_grad).astype(jnp.bfloat16), saved_pre)

    pre_grad = hidden_step(partial_back, backward_finish)[0]
    entry_grad = jnp.einsum(
        "upj,uoj->upo",
        pre_grad.reshape(2, experts * CAP, FF),
        w_in_local,
        preferred_element_type=jnp.float32,
    ).astype(jnp.bfloat16)
    grad_back = collect(entry_grad.reshape(2, experts, CAP, width_local)).reshape(
        slot_total, width_local
    )
    normed_grad = router_grad + jnp.einsum(
        "ts,sd->td", token_table, grad_back, preferred_element_type=jnp.float32
    )
    norm_dot = row_total(jnp.sum(normed_grad * scaled, axis=1))[:, None]
    state_grad = (
        grad_wide
        + inv_rms * norm_gain[None, :] * normed_grad
        - inv_rms**3 / D * state_wide * norm_dot
    )
    return (layer_out, state_grad.astype(jnp.bfloat16))


def solution(mesh):
    in_specs = (
        P("seq", "grp"),
        P("seq", "grp"),
        P("seq", "grp"),
        P("seq", "grp"),
        P(),
        P("seq"),
        P("seq", None),
        P("grp"),
        P("grp", None),
        P(None, "seq", "grp", None),
        P(None, "seq", None, "grp"),
        P("seq", "grp"),
    )
    out_specs = (P("seq", "grp"), P("seq", "grp"))
    return jax.shard_map(body, mesh=mesh, in_specs=in_specs, out_specs=out_specs, check_vma=False)
```

profile of v0, /device:TPU:1, one launch (start us, length us, event | category | flops | bytes accessed | tf_op | source)
XLA Modules:
  0.0 651.5 jit_solution(6634678139856003361)
XLA Ops:
  13.0 2.5 fusion.34
  15.5 79.9 %all-gather.3.cloned.1.call-done = bf16[4096,128]{1,0:T(8,128)(2,1)} async-done(((bf16[128,128]{1,0:T(8,128)(2,1)}), bf16[4096,128]{1,0:T(8,128)(2,1)}) %all-gather.3.cloned.1.call-update) | async-done | bytes 1048592 | tf_op jit(solution)/shard_map/all_gather | solution.py:47
  95.4 3.8 fusion.2
  99.2 5.7 copy-done.2
  104.9 4.0 fusion.3
  109.0 68.1 %all-gather.5.cloned.1.call-done = bf16[4096,128]{0,1:T(8,128)(2,1)} async-done(((bf16[128,128]{0,1:T(8,128)(2,1)}), bf16[4096,128]{0,1:T(8,128)(2,1)}) %all-gather.5.cloned.1.call-update) | async-done | bytes 1048592 | tf_op jit(solution)/shard_map/all_gather | solution.py:48
  177.2 12.9 %fusion.71 = f32[1,128,128,8]{2,1,3,0:T(8,128)S(1)} fusion(bf16[4096,128]{0,1:T(8,128)(2,1)} %all-gather.5.cloned.1.call-done, f32[4096,128,8]{1,0,2:T(8,128)} %copy-done.2, f32[128,8]{0,1:T(8,128)S(1)} %broadcast_maximum_fusion, pred[128,4096]{0,1:T(8,128)(4,1)S(1)} %fusion.34, f32[128,8]{0,1:T(8,128)S(1)} %fusion.3), kind=kOutput, calls=%fused_computation.69 | convolution fusion | flops 6459621376 | bytes 18882560 | tf_op jit(solution)/shard_map/qhgk,khd->qhgd/dot_general | solution.py:64
  190.5 15.0 %psum.42 = f32[128]{0:T(128)S(1)} all-reduce(f32[128]{0:T(128)S(1)} %get-tuple-element.6), channel_id=1, replica_groups=mesh['seq'=32,'grp'=8] {'grp'}, use_global_device_ids=true, to_apply=%region_3.4 | all-reduce | flops 128 | bytes 1024 | tf_op jit(solution)/shard_map/psum | solution.py:22
  205.8 22.5 %psum.43 = f32[128,64]{0,1:T(8,128)S(1)} all-reduce(f32[128,64]{0,1:T(8,128)S(1)} %fusion.92), channel_id=1, replica_groups=mesh['seq'=32,'grp'=8] {'grp'}, use_global_device_ids=true, to_apply=%region_4.5 | all-reduce | flops 8192 | bytes 65536 | tf_op jit(solution)/shard_map/psum | solution.py:22
  231.5 6.3 all-to-all-start.2
  240.1 47.7 %all-to-all-done.2 = bf16[2,32,16,1024]{3,2,0,1:T(8,128)(2,1)S(1)} async-done(((bf16[2,32,16,1024]{3,2,0,1:T(8,128)(2,1)}), bf16[2,32,16,1024]{3,2,0,1:T(8,128)(2,1)S(1)}, u32[]{:S(2)}, u32[]{:S(2)}) %all-to-all-start.2) | async-done | bytes 2097184 | tf_op jit(solution)/shard_map/all_to_all | solution.py:26
  287.8 8.5 %all-to-all-start = ((bf16[2,32,16,1024]{3,2,0,1:T(8,128)(2,1)}), bf16[2,32,16,1024]{3,2,0,1:T(8,128)(2,1)}, u32[]{:S(2)}, u32[]{:S(2)}) async-start(bf16[2,32,16,1024]{3,2,0,1:T(8,128)(2,1)} %copy.82), calls=%async_computation | async-start | bytes 4194304 | tf_op jit(solution)/shard_map/all_to_all | solution.py:26
  296.7 7.5 %fusion.31 = bf16[2,512,1408]{2,1,0:T(8,128)(2,1)} fusion(bf16[2,512,1024]{2,1,0:T(8,128)(2,1)S(1)} %bitcast.131, bf16[2,1,1408,1024]{3,2,1,0:T(8,128)(2,1)} %param.22), kind=kOutput, calls=%fused_computation.38 | convolution fusion | flops 2954231808 | bytes 10747904 | tf_op jit(solution)/shard_map/ukx,utx->ukt/dot_general | solution.py:165
  304.2 40.7 %all-to-all-done = bf16[2,32,16,1024]{3,2,0,1:T(8,128)(2,1)} async-done(((bf16[2,32,16,1024]{3,2,0,1:T(8,128)(2,1)}), bf16[2,32,16,1024]{3,2,0,1:T(8,128)(2,1)}, u32[]{:S(2)}, u32[]{:S(2)}) %all-to-all-start) | async-done | bytes 2097184 | tf_op jit(solution)/shard_map/all_to_all | solution.py:26
  346.7 7.4 %fusion.28 = bf16[2,512,1408]{2,1,0:T(8,128)(2,1)} fusion(bf16[2,512,1024]{2,1,0:T(8,128)(2,1)S(1)} %bitcast.132, bf16[2,1,1024,1408]{3,2,1,0:T(8,128)(2,1)} %param.21), kind=kOutput, calls=%fused_computation.37 | convolution fusion | flops 2954231808 | bytes 10747904 | tf_op jit(solution)/shard_map/ohn,ons->ohs/dot_general | solution.py:125
  354.1 135.9 %all-reduce.3.cloned.1.call-done = (bf16[2,32,16,1408]{3,2,1,0:T(8,128)(2,1)}, bf16[2,32,16,1408]{3,2,1,0:T(8,128)(2,1)}) async-done(((bf16[2,32,16,1408]{3,2,1,0:T(8,128)(2,1)}, bf16[2,32,16,1408]{3,2,1,0:T(8,128)(2,1)}), (bf16[2,32,16,1408]{3,2,1,0:T(8,128)(2,1)}, bf16[2,32,16,1408]{3,2,1,0:T(8,128)(2,1)})) %all-reduce.3.cloned.1.call-update) | async-done | bytes 5767184 | tf_op jit(solution)/shard_map/psum | solution.py:34
  490.0 7.6 %fusion.12 = (bf16[2,32,16,1408]{3,2,1,0:T(8,128)(2,1)}, bf16[2,32,16,1408]{3,2,1,0:T(8,128)(2,1)S(1)}) fusion(bf16[2,32,16,1408]{3,2,1,0:T(8,128)(2,1)} %get-tuple-element.5, bf16[2,32,16,1408]{3,2,1,0:T(8,128)(2,1)} %get-tuple-element.4), kind=kLoop, calls=%fused_computation.20 | loop fusion | flops 34603008 | bytes 11534336 | tf_op jit(solution)/shard_map/convert_element_type | solution.py:173
  497.6 3.7 fusion.46
  503.0 11.7 %all-to-all-start.1 = ((bf16[2,32,16,1024]{3,2,0,1:T(8,128)(2,1)}), bf16[2,32,16,1024]{3,2,0,1:T(8,128)(2,1)S(1)}, u32[]{:S(2)}, u32[]{:S(2)}) async-start(bf16[2,32,16,1024]{3,2,0,1:T(8,128)(2,1)} %copy.84), calls=%async_computation.1 | async-start | bytes 4194304 | tf_op jit(solution)/shard_map/all_to_all | solution.py:30
  514.6 7.0 %fusion.43 = bf16[2,512,1024]{2,1,0:T(8,128)(2,1)S(1)} fusion(bf16[2,512,1408]{2,1,0:T(8,128)(2,1)} %bitcast.128, bf16[2,1,1024,1408]{3,2,1,0:T(8,128)(2,1)} %param.21), kind=kOutput, calls=%fused_computation.51 | convolution fusion | flops 2953838592 | bytes 10747904 | tf_op jit(solution)/shard_map/upj,uoj->upo/dot_general | solution.py:176
  523.3 39.5 %all-to-all-done.1 = bf16[2,32,16,1024]{3,2,0,1:T(8,128)(2,1)S(1)} async-done(((bf16[2,32,16,1024]{3,2,0,1:T(8,128)(2,1)}), bf16[2,32,16,1024]{3,2,0,1:T(8,128)(2,1)S(1)}, u32[]{:S(2)}, u32[]{:S(2)}) %all-to-all-start.1) | async-done | bytes 2097184 | tf_op jit(solution)/shard_map/all_to_all | solution.py:30
  564.1 7.0 %all-to-all-start.3 = ((bf16[2,32,16,1024]{3,2,0,1:T(8,128)(2,1)}), bf16[2,32,16,1024]{3,2,0,1:T(8,128)(2,1)S(1)}, u32[]{:S(2)}, u32[]{:S(2)}) async-start(bf16[2,32,16,1024]{3,2,0,1:T(8,128)(2,1)} %copy.88), calls=%async_computation.3 | async-start | bytes 4194304 | tf_op jit(solution)/shard_map/all_to_all | solution.py:30
  575.1 50.6 %psum.45 = f32[128,4]{0,1:T(4,128)S(1)} all-reduce(f32[128,4]{0,1:T(4,128)S(1)} %get-tuple-element.2), channel_id=1, replica_groups=mesh['seq'=32,'grp'=8] {'grp'}, use_global_device_ids=true, to_apply=%region_12.13 | all-reduce | flops 512 | bytes 4096 | tf_op jit(solution)/shard_map/psum | solution.py:22
  627.0 15.9 %psum.47 = f32[128]{0:T(128)S(1)} all-reduce(f32[128]{0:T(128)S(1)} %get-tuple-element.18), channel_id=1, replica_groups=mesh['seq'=32,'grp'=8] {'grp'}, use_global_device_ids=true, to_apply=%region_17.18 | all-reduce | flops 128 | bytes 1024 | tf_op jit(solution)/shard_map/psum | solution.py:22
  (70 shorter events, 26.1 us)
Async XLA Ops:
  7.2 88.2 %copy-start = (bf16[128,1024]{1,0:T(8,128)(2,1)S(1)}, bf16[128,1024]{1,0:T(8,128)(2,1)}, u32[]{:S(2)}) copy-start(bf16[128,1024]{1,0:T(8,128)(2,1)} %param.13) | copy-start | bytes 786436
  7.2 88.2 %all-gather.3.cloned.1.call-start = ((), (), s32[]{:S(2)}) async-start(), calls=%async_computation.4 | async-start | bytes 1081344 | tf_op jit(solution)/shard_map/all_gather | solution.py:47
  7.9 169.2 %all-gather.5.cloned.1.call-start = ((), (), s32[]{:S(2)}) async-start(), calls=%async_computation.5 | async-start | bytes 1081344 | tf_op jit(solution)/shard_map/all_gather | solution.py:48
  99.2 5.7 copy-start.2
  109.0 81.3 %copy-start.5 = (bf16[128,1024]{1,0:T(8,128)(2,1)S(1)}, bf16[128,1024]{1,0:T(8,128)(2,1)}, u32[]{:S(2)}) copy-start(bf16[128,1024]{1,0:T(8,128)(2,1)} %param.12) | copy-start | bytes 786436
  109.0 96.5 %copy-start.6 = (bf16[1024,64]{0,1:T(8,128)(2,1)S(1)}, bf16[1024,64]{0,1:T(8,128)(2,1)}, u32[]{:S(2)}) copy-start(bf16[1024,64]{0,1:T(8,128)(2,1)} %param.20) | copy-start | bytes 393220
  109.0 96.5 %copy-start.7 = (f32[1024]{0:T(1024)S(1)}, f32[1024]{0:T(1024)}, u32[]{:S(2)}) copy-start(f32[1024]{0:T(1024)} %param.19) | copy-start | bytes 12292
  109.0 120.3 %copy-start.4 = (bf16[128,1024]{1,0:T(8,128)(2,1)S(1)}, bf16[128,1024]{1,0:T(8,128)(2,1)}, u32[]{:S(2)}) copy-start(bf16[128,1024]{1,0:T(8,128)(2,1)} %param.23) | copy-start | bytes 786436
  231.5 56.3 %all-to-all-start.2 = ((bf16[2,32,16,1024]{3,2,0,1:T(8,128)(2,1)}), bf16[2,32,16,1024]{3,2,0,1:T(8,128)(2,1)S(1)}, u32[]{:S(2)}, u32[]{:S(2)}) async-start(bf16[2,32,16,1024]{3,2,0,1:T(8,128)(2,1)} %copy.86), calls=%async_computation.2 | async-start | bytes 4194304 | tf_op jit(solution)/shard_map/all_to_all | solution.py:26
  287.8 57.0 %all-to-all-start = ((bf16[2,32,16,1024]{3,2,0,1:T(8,128)(2,1)}), bf16[2,32,16,1024]{3,2,0,1:T(8,128)(2,1)}, u32[]{:S(2)}, u32[]{:S(2)}) async-start(bf16[2,32,16,1024]{3,2,0,1:T(8,128)(2,1)} %copy.82), calls=%async_computation | async-start | bytes 4194304 | tf_op jit(solution)/shard_map/all_to_all | solution.py:26
  296.4 193.6 %all-reduce.3.cloned.1.call-start = ((), (), s32[]{:S(2)}) async-start(), calls=%async_computation.6 | async-start | bytes 11534336 | tf_op jit(solution)/shard_map/psum | solution.py:34
  354.1 143.5 %slice-start = ((s8[5767168]{0:T(1024)(128)(4,1)}), s8[1572864]{0:T(1024)(128)(4,1)S(1)}, s32[]{:S(2)}) async-start(s8[5767168]{0:T(1024)(128)(4,1)} %bitcast.138), calls=%async_computation.7 | async-start | bytes 3145728
  490.0 7.6 %slice-start.1 = ((s8[5767168]{0:T(1024)(128)(4,1)}), s8[4194304]{0:T(1024)(128)(4,1)S(1)}, s32[]{:S(2)}) async-start(s8[5767168]{0:T(1024)(128)(4,1)} %bitcast.138), calls=%async_computation.8 | async-start | bytes 8388608
  503.0 59.8 %all-to-all-start.1 = ((bf16[2,32,16,1024]{3,2,0,1:T(8,128)(2,1)}), bf16[2,32,16,1024]{3,2,0,1:T(8,128)(2,1)S(1)}, u32[]{:S(2)}, u32[]{:S(2)}) async-start(bf16[2,32,16,1024]{3,2,0,1:T(8,128)(2,1)} %copy.84), calls=%async_computation.1 | async-start | bytes 4194304 | tf_op jit(solution)/shard_map/all_to_all | solution.py:30
  562.8 1.3 copy-start.3
  564.1 61.7 %all-to-all-start.3 = ((bf16[2,32,16,1024]{3,2,0,1:T(8,128)(2,1)}), bf16[2,32,16,1024]{3,2,0,1:T(8,128)(2,1)S(1)}, u32[]{:S(2)}, u32[]{:S(2)}) async-start(bf16[2,32,16,1024]{3,2,0,1:T(8,128)(2,1)} %copy.88), calls=%async_computation.3 | async-start | bytes 4194304 | tf_op jit(solution)/shard_map/all_to_all | solution.py:30
  625.8 19.2 %copy-start.1 = (bf16[128,1024]{1,0:T(8,128)(2,1)S(1)}, bf16[128,1024]{1,0:T(8,128)(2,1)}, u32[]{:S(2)}) copy-start(bf16[128,1024]{1,0:T(8,128)(2,1)} %param.13) | copy-start | bytes 786436
Sparse Core Ops, SparseCore 0:
  11.4 83.9 all-gather.2
  99.2 77.9 all-gather.4
  354.2 135.7 all-reduce.2
where the time goes:
time: 652 us
  waiting for transfers between devices  413 us (63%)
  blocking collectives  104 us (16%)
  matrix products  48.5 us (7%)
  starting transfers between devices  33.5 us (5%)
  local copies, waits for them, and re-layouts  20.5 us (3%)
  other arithmetic  18.4 us (3%)
  between operations  14 us (2%)
    psum x1, waiting for transfers between devices, hidden_step(): lax.psum(partial_value.astype(jnp.bfloat16), 'grp').astype(jnp.float32)  136 us
    psum x4, blocking collectives, row_total(): return lax.psum(partial_value, 'grp')  104 us
    all_to_all x2, waiting for transfers between devices, dispatch(): lax.all_to_all(buffers, 'seq', split_axis=1, concat_axis=1, tiled=True)  88.4 us
    all_gather x1, waiting for transfers between devices, attend(): key_piece = lax.all_gather(key_states, 'seq', axis=0, tiled=True)  79.9 us
    all_gather x1, waiting for transfers between devices, attend(): value_piece = lax.all_gather(value_states, 'seq', axis=0, tiled=True)  68.1 us
    all_to_all x2, waiting for transfers between devices, collect(): lax.all_to_all(buffers, 'seq', split_axis=1, concat_axis=1, tiled=True)  39.5 us
    all_to_all x2, starting transfers between devices, collect(): lax.all_to_all(buffers, 'seq', split_axis=1, concat_axis=1, tiled=True)  18.6 us
    all_to_all x2, starting transfers between devices, dispatch(): lax.all_to_all(buffers, 'seq', split_axis=1, concat_axis=1, tiled=True)  14.8 us
  transfers between devices with their start and end apart: 7, of which 6 were waited for; matrix products, arithmetic and copies ran while one was open for 6% of the time, Pallas kernels for 0%

commit v1 on v0

--- a/solution.py
+++ b/solution.py
@@ -44,8 +44,13 @@
     query_pos = first_query + jnp.arange(length, dtype=jnp.int32)
     query_doc = lax.dynamic_slice_in_dim(doc_ids, first_query, length)
     score_scale = HEAD_DIM ** (-0.5)
-    key_piece = lax.all_gather(key_states, "seq", axis=0, tiled=True)
-    value_piece = lax.all_gather(value_states, "seq", axis=0, tiled=True)
+    key_piece, value_piece = jnp.split(
+        lax.all_gather(
+            jnp.concatenate([key_states, value_states], axis=1), "seq", axis=0, tiled=True
+        ),
+        [key_states.shape[1]],
+        axis=1,
+    )
     piece_rows = key_piece.shape[0]
     best_score = jnp.full((length, kv_local, group_size), -1e30, jnp.float32)
     key_heads = key_piece.reshape(piece_rows, kv_local, HEAD_DIM)

time: 652 us -> 585 us (0.90)
  waiting for transfers between devices: 413 us -> 355 us
  local copies, waits for them, and re-layouts: 20.5 us -> 13.3 us
    all_gather x2 -> x1, waiting for transfers between devices: 148 us -> 91.4 us  [attend(): lax.all_gather(jnp.concatenate([key_states, value_states], axis=1), 'seq'...]
    unnamed x21 -> x20, local copies, waits for them, and re-layouts: 8.51 us -> 1.35 us
  transfers between devices with their start and end apart: 7 -> 6, of which waited for: 6 -> 5; matrix products, arithmetic and copies ran while one was open for 6% -> 5% of each run, Pallas kernels for 0% -> 0%
where the time goes in v1:
time: 585 us; the launch traced here: 584 us
  waiting for transfers between devices  355 us (61%)
  blocking collectives  105 us (18%)
  matrix products  45.1 us (8%)
  starting transfers between devices  31.9 us (5%)
  other arithmetic  20.1 us (3%)
  between operations  14.3 us (2%)
  local copies, waits for them, and re-layouts  13.3 us (2%)
    psum x1, waiting for transfers between devices, hidden_step(): lax.psum(partial_value.astype(jnp.bfloat16), 'grp').astype(jnp.float32)  136 us
    psum x4, blocking collectives, row_total(): return lax.psum(partial_value, 'grp')  105 us
    all_gather x1, waiting for transfers between devices, attend(): lax.all_gather(jnp.concatenate([key_states, value_states], axis=1), 'seq'...  91.4 us
    all_to_all x2, waiting for transfers between devices, dispatch(): lax.all_to_all(buffers, 'seq', split_axis=1, concat_axis=1, tiled=True)  88.4 us
    all_to_all x2, waiting for transfers between devices, collect(): lax.all_to_all(buffers, 'seq', split_axis=1, concat_axis=1, tiled=True)  39.3 us
    all_to_all x2, starting transfers between devices, collect(): lax.all_to_all(buffers, 'seq', split_axis=1, concat_axis=1, tiled=True)  18.9 us
    all_to_all x2, starting transfers between devices, dispatch(): lax.all_to_all(buffers, 'seq', split_axis=1, concat_axis=1, tiled=True)  12.9 us
  transfers between devices with their start and end apart: 6, of which 5 were waited for; matrix products, arithmetic and copies ran while one was open for 5% of the time, Pallas kernels for 0%

profile of v1, /device:TPU:1, one launch (start us, length us, event | category | flops | bytes accessed | tf_op | source)
XLA Modules:
  0.0 584.2 jit_solution(624936445112518706)
XLA Ops:
  12.3 2.5 fusion.34
  14.8 91.4 %all-gather.2.cloned.1.call-done = bf16[4096,256]{1,0:T(8,128)(2,1)} async-done(((bf16[128,256]{1,0:T(8,128)(2,1)}), bf16[4096,256]{1,0:T(8,128)(2,1)}) %all-gather.2.cloned.1.call-update) | async-done | bytes 2097168 | tf_op jit(solution)/shard_map/all_gather | solution.py:48
  106.1 3.8 fusion.2
  110.0 4.2 fusion.3
  114.3 9.5 %fusion.65 = f32[1,128,128,8]{2,1,3,0:T(8,128)S(1)} fusion(f32[4096,128,8]{1,0,2:T(8,128)S(1)} %get-tuple-element.17, f32[128,8]{0,1:T(8,128)S(1)} %broadcast_maximum_fusion, pred[128,4096]{0,1:T(8,128)(4,1)S(1)} %fusion.34, bf16[4096,256]{1,0:T(8,128)(2,1)S(1)} %copy-done.7, f32[128,8]{0,1:T(8,128)S(1)} %fusion.3), kind=kOutput, calls=%fused_computation.69 | convolution fusion | flops 6459621376 | bytes 18882560 | tf_op jit(solution)/shard_map/qhgk,khd->qhgd/dot_general | solution.py:69
  124.2 15.3 %psum.42 = f32[128]{0:T(128)S(1)} all-reduce(f32[128]{0:T(128)S(1)} %get-tuple-element.6), channel_id=1, replica_groups=mesh['seq'=32,'grp'=8] {'grp'}, use_global_device_ids=true, to_apply=%region_3.4 | all-reduce | flops 128 | bytes 1024 | tf_op jit(solution)/shard_map/psum | solution.py:22
  139.7 22.8 %psum.43 = f32[128,64]{0,1:T(8,128)S(1)} all-reduce(f32[128,64]{0,1:T(8,128)S(1)} %fusion.84), channel_id=1, replica_groups=mesh['seq'=32,'grp'=8] {'grp'}, use_global_device_ids=true, to_apply=%region_4.5 | all-reduce | flops 8192 | bytes 65536 | tf_op jit(solution)/shard_map/psum | solution.py:22
  165.8 4.4 all-to-all-start.2
  172.5 47.8 %all-to-all-done.2 = bf16[2,32,16,1024]{3,2,0,1:T(8,128)(2,1)S(1)} async-done(((bf16[2,32,16,1024]{3,2,0,1:T(8,128)(2,1)}), bf16[2,32,16,1024]{3,2,0,1:T(8,128)(2,1)S(1)}, u32[]{:S(2)}, u32[]{:S(2)}) %all-to-all-start.2) | async-done | bytes 2097184 | tf_op jit(solution)/shard_map/all_to_all | solution.py:26
  220.2 8.5 %all-to-all-start = ((bf16[2,32,16,1024]{3,2,0,1:T(8,128)(2,1)}), bf16[2,32,16,1024]{3,2,0,1:T(8,128)(2,1)}, u32[]{:S(2)}, u32[]{:S(2)}) async-start(bf16[2,32,16,1024]{3,2,0,1:T(8,128)(2,1)} %copy.82), calls=%async_computation | async-start | bytes 4194304 | tf_op jit(solution)/shard_map/all_to_all | solution.py:26
  229.1 7.5 %fusion.31 = bf16[2,512,1408]{2,1,0:T(8,128)(2,1)} fusion(bf16[2,512,1024]{2,1,0:T(8,128)(2,1)S(1)} %bitcast.129, bf16[2,1,1408,1024]{3,2,1,0:T(8,128)(2,1)} %param.22), kind=kOutput, calls=%fused_computation.38 | convolution fusion | flops 2954231808 | bytes 10747904 | tf_op jit(solution)/shard_map/ukx,utx->ukt/dot_general | solution.py:170
  236.6 40.7 %all-to-all-done = bf16[2,32,16,1024]{3,2,0,1:T(8,128)(2,1)} async-done(((bf16[2,32,16,1024]{3,2,0,1:T(8,128)(2,1)}), bf16[2,32,16,1024]{3,2,0,1:T(8,128)(2,1)}, u32[]{:S(2)}, u32[]{:S(2)}) %all-to-all-start) | async-done | bytes 2097184 | tf_op jit(solution)/shard_map/all_to_all | solution.py:26
  279.1 7.4 %fusion.28 = bf16[2,512,1408]{2,1,0:T(8,128)(2,1)} fusion(bf16[2,512,1024]{2,1,0:T(8,128)(2,1)S(1)} %bitcast.130, bf16[2,1,1024,1408]{3,2,1,0:T(8,128)(2,1)} %param.21), kind=kOutput, calls=%fused_computation.37 | convolution fusion | flops 2954231808 | bytes 10747904 | tf_op jit(solution)/shard_map/ohn,ons->ohs/dot_general | solution.py:130
  286.5 135.9 %all-reduce.3.cloned.1.call-done = (bf16[2,32,16,1408]{3,2,1,0:T(8,128)(2,1)}, bf16[2,32,16,1408]{3,2,1,0:T(8,128)(2,1)}) async-done(((bf16[2,32,16,1408]{3,2,1,0:T(8,128)(2,1)}, bf16[2,32,16,1408]{3,2,1,0:T(8,128)(2,1)}), (bf16[2,32,16,1408]{3,2,1,0:T(8,128)(2,1)}, bf16[2,32,16,1408]{3,2,1,0:T(8,128)(2,1)})) %all-reduce.3.cloned.1.call-update) | async-done | bytes 5767184 | tf_op jit(solution)/shard_map/psum | solution.py:34
  422.4 7.6 %fusion.12 = (bf16[2,32,16,1408]{3,2,1,0:T(8,128)(2,1)}, bf16[2,32,16,1408]{3,2,1,0:T(8,128)(2,1)S(1)}) fusion(bf16[2,32,16,1408]{3,2,1,0:T(8,128)(2,1)} %get-tuple-element.5, bf16[2,32,16,1408]{3,2,1,0:T(8,128)(2,1)} %get-tuple-element.4), kind=kLoop, calls=%fused_computation.20 | loop fusion | flops 34603008 | bytes 11534336 | tf_op jit(solution)/shard_map/convert_element_type | solution.py:178
  430.0 3.7 fusion.46
  435.4 11.9 %all-to-all-start.1 = ((bf16[2,32,16,1024]{3,2,0,1:T(8,128)(2,1)}), bf16[2,32,16,1024]{3,2,0,1:T(8,128)(2,1)S(1)}, u32[]{:S(2)}, u32[]{:S(2)}) async-start(bf16[2,32,16,1024]{3,2,0,1:T(8,128)(2,1)} %copy.84), calls=%async_computation.1 | async-start | bytes 4194304 | tf_op jit(solution)/shard_map/all_to_all | solution.py:30
  447.3 7.0 %fusion.43 = bf16[2,512,1024]{2,1,0:T(8,128)(2,1)S(1)} fusion(bf16[2,512,1408]{2,1,0:T(8,128)(2,1)} %bitcast.126, bf16[2,1,1024,1408]{3,2,1,0:T(8,128)(2,1)} %param.21), kind=kOutput, calls=%fused_computation.51 | convolution fusion | flops 2953838592 | bytes 10747904 | tf_op jit(solution)/shard_map/upj,uoj->upo/dot_general | solution.py:181
  455.9 39.3 %all-to-all-done.1 = bf16[2,32,16,1024]{3,2,0,1:T(8,128)(2,1)S(1)} async-done(((bf16[2,32,16,1024]{3,2,0,1:T(8,128)(2,1)}), bf16[2,32,16,1024]{3,2,0,1:T(8,128)(2,1)S(1)}, u32[]{:S(2)}, u32[]{:S(2)}) %all-to-all-start.1) | async-done | bytes 2097184 | tf_op jit(solution)/shard_map/all_to_all | solution.py:30
  496.5 6.9 %all-to-all-start.3 = ((bf16[2,32,16,1024]{3,2,0,1:T(8,128)(2,1)}), bf16[2,32,16,1024]{3,2,0,1:T(8,128)(2,1)S(1)}, u32[]{:S(2)}, u32[]{:S(2)}) async-start(bf16[2,32,16,1024]{3,2,0,1:T(8,128)(2,1)} %copy.88), calls=%async_computation.3 | async-start | bytes 4194304 | tf_op jit(solution)/shard_map/all_to_all | solution.py:30
  505.3 2.2 multiply_reduce_fusion
  507.5 50.6 %psum.45 = f32[128,4]{0,1:T(4,128)S(1)} all-reduce(f32[128,4]{0,1:T(4,128)S(1)} %get-tuple-element.2), channel_id=1, replica_groups=mesh['seq'=32,'grp'=8] {'grp'}, use_global_device_ids=true, to_apply=%region_12.13 | all-reduce | flops 512 | bytes 4096 | tf_op jit(solution)/shard_map/psum | solution.py:22
  559.4 15.9 %psum.47 = f32[128]{0:T(128)S(1)} all-reduce(f32[128]{0:T(128)S(1)} %get-tuple-element.18), channel_id=1, replica_groups=mesh['seq'=32,'grp'=8] {'grp'}, use_global_device_ids=true, to_apply=%region_17.18 | all-reduce | flops 128 | bytes 1024 | tf_op jit(solution)/shard_map/psum | solution.py:22
  575.3 2.1 fusion.76
  (67 shorter events, 21.1 us)
Async XLA Ops:
  7.2 99.0 %copy-start = (bf16[128,1024]{1,0:T(8,128)(2,1)S(1)}, bf16[128,1024]{1,0:T(8,128)(2,1)}, u32[]{:S(2)}) copy-start(bf16[128,1024]{1,0:T(8,128)(2,1)} %param.13) | copy-start | bytes 786436
  7.2 99.0 %all-gather.2.cloned.1.call-start = ((), (), s32[]{:S(2)}) async-start(), calls=%async_computation.4 | async-start | bytes 2162688 | tf_op jit(solution)/shard_map/all_gather | solution.py:48
  110.0 4.3 copy-start.7
  114.2 9.8 %copy-start.4 = (bf16[128,1024]{1,0:T(8,128)(2,1)S(1)}, bf16[128,1024]{1,0:T(8,128)(2,1)}, u32[]{:S(2)}) copy-start(bf16[128,1024]{1,0:T(8,128)(2,1)} %param.12) | copy-start | bytes 786436
  114.2 25.2 %copy-start.5 = (bf16[1024,64]{0,1:T(8,128)(2,1)S(1)}, bf16[1024,64]{0,1:T(8,128)(2,1)}, u32[]{:S(2)}) copy-start(bf16[1024,64]{0,1:T(8,128)(2,1)} %param.20) | copy-start | bytes 393220
  114.2 25.2 %copy-start.6 = (f32[1024]{0:T(1024)S(1)}, f32[1024]{0:T(1024)}, u32[]{:S(2)}) copy-start(f32[1024]{0:T(1024)} %param.19) | copy-start | bytes 12292
  114.3 49.2 %copy-start.3 = (bf16[128,1024]{1,0:T(8,128)(2,1)S(1)}, bf16[128,1024]{1,0:T(8,128)(2,1)}, u32[]{:S(2)}) copy-start(bf16[128,1024]{1,0:T(8,128)(2,1)} %param.23) | copy-start | bytes 786436
  165.8 54.5 %all-to-all-start.2 = ((bf16[2,32,16,1024]{3,2,0,1:T(8,128)(2,1)}), bf16[2,32,16,1024]{3,2,0,1:T(8,128)(2,1)S(1)}, u32[]{:S(2)}, u32[]{:S(2)}) async-start(bf16[2,32,16,1024]{3,2,0,1:T(8,128)(2,1)} %copy.86), calls=%async_computation.2 | async-start | bytes 4194304 | tf_op jit(solution)/shard_map/all_to_all | solution.py:26
  220.2 57.0 %all-to-all-start = ((bf16[2,32,16,1024]{3,2,0,1:T(8,128)(2,1)}), bf16[2,32,16,1024]{3,2,0,1:T(8,128)(2,1)}, u32[]{:S(2)}, u32[]{:S(2)}) async-start(bf16[2,32,16,1024]{3,2,0,1:T(8,128)(2,1)} %copy.82), calls=%async_computation | async-start | bytes 4194304 | tf_op jit(solution)/shard_map/all_to_all | solution.py:26
  228.7 193.6 %all-reduce.3.cloned.1.call-start = ((), (), s32[]{:S(2)}) async-start(), calls=%async_computation.5 | async-start | bytes 11534336 | tf_op jit(solution)/shard_map/psum | solution.py:34
  286.5 143.5 %slice-start = ((s8[5767168]{0:T(1024)(128)(4,1)}), s8[1572864]{0:T(1024)(128)(4,1)S(1)}, s32[]{:S(2)}) async-start(s8[5767168]{0:T(1024)(128)(4,1)} %bitcast.136), calls=%async_computation.6 | async-start | bytes 3145728
  422.4 7.6 %slice-start.1 = ((s8[5767168]{0:T(1024)(128)(4,1)}), s8[4194304]{0:T(1024)(128)(4,1)S(1)}, s32[]{:S(2)}) async-start(s8[5767168]{0:T(1024)(128)(4,1)} %bitcast.136), calls=%async_computation.7 | async-start | bytes 8388608
  435.4 59.9 %all-to-all-start.1 = ((bf16[2,32,16,1024]{3,2,0,1:T(8,128)(2,1)}), bf16[2,32,16,1024]{3,2,0,1:T(8,128)(2,1)S(1)}, u32[]{:S(2)}, u32[]{:S(2)}) async-start(bf16[2,32,16,1024]{3,2,0,1:T(8,128)(2,1)} %copy.84), calls=%async_computation.1 | async-start | bytes 4194304 | tf_op jit(solution)/shard_map/all_to_all | solution.py:30
  495.3 1.3 copy-start.2
  496.5 61.6 %all-to-all-start.3 = ((bf16[2,32,16,1024]{3,2,0,1:T(8,128)(2,1)}), bf16[2,32,16,1024]{3,2,0,1:T(8,128)(2,1)S(1)}, u32[]{:S(2)}, u32[]{:S(2)}) async-start(bf16[2,32,16,1024]{3,2,0,1:T(8,128)(2,1)} %copy.88), calls=%async_computation.3 | async-start | bytes 4194304 | tf_op jit(solution)/shard_map/all_to_all | solution.py:30
  558.2 19.2 %copy-start.1 = (bf16[128,1024]{1,0:T(8,128)(2,1)S(1)}, bf16[128,1024]{1,0:T(8,128)(2,1)}, u32[]{:S(2)}) copy-start(bf16[128,1024]{1,0:T(8,128)(2,1)} %param.13) | copy-start | bytes 786436
Sparse Core Ops, SparseCore 0:
  12.1 93.9 all-gather.1
  286.6 135.7 all-reduce.2
